TPU v7x, 32 devices: a whole 2x2x4 slice. The times are simulated.
32 devices in a mesh: node: 2 (over x), tm: 4 (over z), space: 4 (over y, core).
Axes of the slice: x: 2, y: 2, z: 4, core: 2. Of those that a mesh axis runs over, the one named last changes fastest.
Arguments:
- nodes: float32 [4, 4, 32, 256, 256], P('tm', 'node', 'space'), may hold values from -1.5 to 1.5
- prev_final: float32 [4, 32, 256, 256], P('tm', 'space'), may hold values from -6 to 6
- u_init: float32 [32, 256, 256], P('space'), may hold values from -6 to 6
- conductivity: float32 [32, 256, 256], P('space'), may hold values from 0.25 to 16
Outputs:
- new_nodes: float32 [4, 4, 32, 256, 256], P('tm', 'node', 'space')
All inputs are finite; a program needn't handle non-finite values.
Results may differ from a plain program's by a relative error of at most 0.0003.
Values sent between devices are 32-bit elements; how exact they have to be, the bound alone decides.
A program may use at most 128 MiB of HBM per device.

v0:
```python
import functools

import jax
import jax.numpy as jnp
from jax import lax
from jax.experimental import pallas as pl
from jax.experimental.pallas import tpu as pltpu
from jax.sharding import PartitionSpec as P

SWEEPS = 8
ROWS = 16
PAD = 8
MESH = pl.DeviceIdType.MESH

radau_points = [0.08858795951270394, 0.4094668644407347, 0.787659461760847, 1.0]


def mixing_table():
    count_nodes = len(radau_points)
    table = [[0.0] * count_nodes for row_index in range(count_nodes)]
    for column in range(count_nodes):
        coefs = [1.0]
        for other in range(count_nodes):
            if other != column:
                scale = 1.0 / (radau_points[column] - radau_points[other])
                shifted = [0.0] + coefs
                lowered = [value * radau_points[other] for value in coefs] + [0.0]
                coefs = [(shifted[k] - lowered[k]) * scale for k in range(len(shifted))]
        for row_index in range(count_nodes):
            point = radau_points[row_index]
            integral = 0.0
            for power in range(len(coefs)):
                integral = integral + coefs[power] * point ** (power + 1) / (power + 1)
            table[row_index][column] = integral
        table[column][column] = table[column][column] - radau_points[column]
    return table


def pick(position, values):
    result = jnp.float32(values[0])
    for k in range(1, len(values)):
        result = jnp.where(position == k, jnp.float32(values[k]), result)
    return result


def kernel(
    sizes, nodes, prev, init, cond, out,
    own, theirs, start, even, odd, kpad, fx, fyl, fyr, fzl, fzr, inv, rhs, result,
    load_sem, k_send, k_recv, node_send, node_recv, prev_send, prev_recv,
    halo_send, halo_recv, out_sem,
):
    n_node, n_tm, n_space, per, bricks, height = sizes
    chunks = height // ROWS
    node = lax.axis_index("node")
    tm = lax.axis_index("tm")
    space = lax.axis_index("space")
    has_lower = space > 0
    has_upper = space < n_space - 1
    lower = jnp.maximum(space - 1, 0)
    upper = jnp.minimum(space + 1, n_space - 1)
    later = jnp.minimum(tm + 1, n_tm - 1)
    earlier = jnp.maximum(tm - 1, 0)
    first_tm = tm == 0
    last_tm = tm == n_tm - 1
    inner = pl.ds(PAD, height)

    table = mixing_table()
    mix = [
        [
            [
                pick(
                    node,
                    [
                        table[p * per + i][((p + n_node - d) % n_node) * per + j]
                        / radau_points[p * per + i]
                        for p in range(n_node)
                    ],
                )
                for j in range(per)
            ]
            for d in range(n_node)
        ]
        for i in range(per)
    ]
    point = [pick(node, [radau_points[p * per + i] for p in range(n_node)]) for i in range(per)]
    inv_point = [pick(node, [1.0 / radau_points[p * per + i] for p in range(n_node)]) for i in range(per)]

    def k_up():
        return pltpu.make_async_remote_copy(
            cond.at[bricks - 1], kpad.at[0, inner], k_send.at[0], k_recv.at[0],
            device_id={"space": upper}, device_id_type=MESH)

    def k_down():
        return pltpu.make_async_remote_copy(
            cond.at[0], kpad.at[bricks + 1, inner], k_send.at[1], k_recv.at[1],
            device_id={"space": lower}, device_id_type=MESH)

    def k_edge_low():
        return pltpu.make_async_copy(cond.at[0], kpad.at[0, inner], k_recv.at[0])

    def k_edge_high():
        return pltpu.make_async_copy(cond.at[bricks - 1], kpad.at[bricks + 1, inner], k_recv.at[1])

    def node_copy(d, b):
        rows = pl.ds(pl.multiple_of(b * ROWS, ROWS), ROWS)
        return pltpu.make_async_remote_copy(
            nodes.at[0, :, :, rows], theirs.at[d - 1, :, :, rows],
            node_send.at[d - 1, b], node_recv.at[d - 1, b],
            device_id={"node": lax.rem(node + d, n_node)}, device_id_type=MESH)

    def prev_copy(b):
        rows = pl.ds(pl.multiple_of(b * ROWS, ROWS), ROWS)
        return pltpu.make_async_remote_copy(
            prev.at[0, :, rows], start.at[:, rows], prev_send.at[b], prev_recv.at[b],
            device_id={"tm": later}, device_id_type=MESH)

    def init_copy(b):
        rows = pl.ds(pl.multiple_of(b * ROWS, ROWS), ROWS)
        return pltpu.make_async_copy(init.at[:, rows], start.at[:, rows], prev_recv.at[b])

    def halo_up(buffer, s, b):
        rows = pl.ds(pl.multiple_of(PAD + b * ROWS, 8), ROWS)
        return pltpu.make_async_remote_copy(
            buffer.at[:, bricks, rows], buffer.at[:, 0, rows],
            halo_send.at[0, s], halo_recv.at[0, s, b],
            device_id={"space": upper}, device_id_type=MESH)

    def halo_down(buffer, s, b):
        rows = pl.ds(pl.multiple_of(PAD + b * ROWS, 8), ROWS)
        return pltpu.make_async_remote_copy(
            buffer.at[:, 1, rows], buffer.at[:, bricks + 1, rows],
            halo_send.at[1, s], halo_recv.at[1, s, b],
            device_id={"space": lower}, device_id_type=MESH)

    def out_copy(b):
        rows = pl.ds(pl.multiple_of(b * ROWS, ROWS), ROWS)
        return pltpu.make_async_copy(result.at[:, :, rows], out.at[0, :, :, rows], out_sem.at[b])

    own_load = pltpu.make_async_copy(nodes.at[0], own, load_sem.at[0])
    k_load = pltpu.make_async_copy(cond, kpad.at[pl.ds(1, bricks), inner], load_sem.at[1])
    own_load.start()
    k_load.start()

    barrier = pltpu.get_barrier_semaphore()
    partners = [(None, {"node": lax.rem(node + d, n_node)}) for d in range(1, n_node)]
    if n_space > 1:
        partners += [(has_lower, {"space": lower}), (has_upper, {"space": upper})]
    if n_tm > 1:
        partners += [(jnp.logical_not(first_tm), {"tm": earlier}), (jnp.logical_not(last_tm), {"tm": later})]
    for guard, target in partners:
        def greet(target=target):
            pl.semaphore_signal(barrier, inc=1, device_id=target, device_id_type=MESH)
        greet() if guard is None else pl.when(guard)(greet)
    peers = n_node - 1
    if n_space > 1:
        peers = peers + has_lower.astype(jnp.int32) + has_upper.astype(jnp.int32)
    if n_tm > 1:
        peers = peers + (tm > 0).astype(jnp.int32) + (tm < n_tm - 1).astype(jnp.int32)
    pl.semaphore_wait(barrier, peers)

    if n_space > 1:
        pl.when(has_upper)(lambda: k_up().start())
        pl.when(has_lower)(lambda: k_down().start())
    pl.when(jnp.logical_not(has_lower))(lambda: k_edge_low().start())
    pl.when(jnp.logical_not(has_upper))(lambda: k_edge_high().start())

    @pl.loop(0, chunks)
    def _(b):
        for d in range(1, n_node):
            node_copy(d, b).start()
        if n_tm > 1:
            pl.when(jnp.logical_not(last_tm))(lambda: prev_copy(b).start())
        pl.when(first_tm)(lambda: init_copy(b).start())

    width = even.shape[-1]
    for buffer in (even, odd):
        for i in range(per):
            for x in range(bricks + 2):
                buffer[i, x, pl.ds(0, PAD)] = jnp.zeros((PAD, width), jnp.float32)
                buffer[i, x, pl.ds(PAD + height, PAD)] = jnp.zeros((PAD, width), jnp.float32)

        @pl.when(jnp.logical_not(has_lower))
        def _():
            @pl.loop(0, chunks)
            def _(b):
                rows = pl.ds(pl.multiple_of(PAD + b * ROWS, 8), ROWS)
                for i in range(per):
                    buffer[i, 0, rows] = jnp.zeros((ROWS, width), jnp.float32)

        @pl.when(jnp.logical_not(has_upper))
        def _():
            @pl.loop(0, chunks)
            def _(b):
                rows = pl.ds(pl.multiple_of(PAD + b * ROWS, 8), ROWS)
                for i in range(per):
                    buffer[i, bricks + 1, rows] = jnp.zeros((ROWS, width), jnp.float32)

    k_load.wait()
    if n_space > 1:
        pl.when(has_lower)(lambda: k_up().wait_recv())
        pl.when(has_upper)(lambda: k_down().wait_recv())
    pl.when(jnp.logical_not(has_lower))(lambda: k_edge_low().wait())
    pl.when(jnp.logical_not(has_upper))(lambda: k_edge_high().wait())
    for x in range(bricks + 2):
        kpad[x, pl.ds(0, PAD)] = jnp.broadcast_to(kpad[x, pl.ds(PAD, 1)], (PAD, width))
        kpad[x, pl.ds(PAD + height, PAD)] = jnp.broadcast_to(kpad[x, pl.ds(PAD + height - 1, 1)], (PAD, width))
    own_load.wait()

    def first_stage(b):
        r = pl.multiple_of(b * ROWS, ROWS)
        rows = pl.ds(r, ROWS)
        inside = pl.ds(pl.multiple_of(r + PAD, 8), ROWS)
        column = lax.broadcasted_iota(jnp.int32, (ROWS, width), 1)
        at_first = column == 0
        at_last = column == width - 1
        for x in range(bricks):
            window = kpad[x + 1, pl.ds(r, ROWS + 2 * PAD)]
            k = window[PAD : PAD + ROWS]
            xl = 0.5 * (k + kpad[x, inside])
            xr = 0.5 * (k + kpad[x + 2, inside])
            yl = 0.5 * (k + window[PAD - 1 : PAD - 1 + ROWS])
            yr = 0.5 * (k + window[PAD + 1 : PAD + 1 + ROWS])
            zl = 0.5 * (k + jnp.where(at_first, k, pltpu.roll(k, 1, 1)))
            zr = 0.5 * (k + jnp.where(at_last, k, pltpu.roll(k, width - 1, 1)))
            total = xl + xr + yl + yr + zl + zr
            fx[x, rows] = xl
            if x == bricks - 1:
                fx[bricks, rows] = xr
            fyl[x, rows] = yl
            fyr[x, rows] = yr
            fzl[x, rows] = jnp.where(at_first, 0.0, zl)
            fzr[x, rows] = jnp.where(at_last, 0.0, zr)
            for i in range(per):
                inv[i, x, rows] = 1.0 / (inv_point[i] + total)
        for d in range(1, n_node):
            node_copy(d, b).wait_recv()
        pl.when(first_tm)(lambda: init_copy(b).wait())
        if n_tm > 1:
            pl.when(jnp.logical_not(first_tm))(lambda: prev_copy(b).wait_recv())
        for x in range(bricks):
            mine = [own[j, x, rows] for j in range(per)]
            states = [mine] + [[theirs[d - 1, j, x, rows] for j in range(per)] for d in range(1, n_node)]
            begin = start[x, rows]
            for i in range(per):
                q = mix[i][0][0] * states[0][0]
                for d in range(n_node):
                    for j in range(per):
                        if d or j:
                            q = q + mix[i][d][j] * states[d][j]
                even[i, x + 1, inside] = mine[i] + q
                rhs[i, x, rows] = (begin + q) * inv_point[i]

    def sweep(src, dst, b, last):
        r = pl.multiple_of(b * ROWS, ROWS)
        rows = pl.ds(r, ROWS)
        inside = pl.ds(pl.multiple_of(r + PAD, 8), ROWS)
        for x in range(bricks):
            xl, xr = fx[x, rows], fx[x + 1, rows]
            yl, yr = fyl[x, rows], fyr[x, rows]
            zl, zr = fzl[x, rows], fzr[x, rows]
            for i in range(per):
                window = src[i, x + 1, pl.ds(r, ROWS + 2 * PAD)]
                centre = window[PAD : PAD + ROWS]
                right = rhs[i, x, rows]
                value = xl * src[i, x, inside] + xr * src[i, x + 2, inside]
                value = value + yl * window[PAD - 1 : PAD - 1 + ROWS]
                value = value + yr * window[PAD + 1 : PAD + 1 + ROWS]
                value = value + zl * pltpu.roll(centre, 1, 1)
                value = value + zr * pltpu.roll(centre, width - 1, 1)
                value = (value + right) * inv[i, x, rows]
                if last:
                    result[i, x, rows] = value - (point[i] * right - start[x, rows])
                else:
                    dst[i, x + 1, inside] = value

    def receive(buffer, s, b):
        if n_space > 1:
            pl.when(has_lower)(lambda: halo_up(buffer, s, b).wait_recv())
            pl.when(has_upper)(lambda: halo_down(buffer, s, b).wait_recv())

    def send(buffer, s, b):
        if n_space > 1:
            @pl.when(has_upper)
            def _():
                pl.when(b > 0)(lambda: halo_up(buffer, s, b - 1).wait_send())
                halo_up(buffer, s, b).start()

            @pl.when(has_lower)
            def _():
                pl.when(b > 0)(lambda: halo_down(buffer, s, b - 1).wait_send())
                halo_down(buffer, s, b).start()

    def settle(buffer, s):
        if n_space > 1:
            pl.when(has_upper)(lambda: halo_up(buffer, s, chunks - 1).wait_send())
            pl.when(has_lower)(lambda: halo_down(buffer, s, chunks - 1).wait_send())

    def stage(src, dst, s, t, last=False):
        b = t - 2 * s

        @pl.when((b >= 0) & (b < chunks))
        def _():
            receive(src, s - 1, b)
            sweep(src, dst, b, last)
            if last:
                out_copy(b).start()
            else:
                send(dst, s, b)

        if not last:
            pl.when(b == chunks)(lambda: settle(dst, s))

    pairs = SWEEPS // 2

    @pl.loop(0, chunks + 2 * SWEEPS)
    def _(t):
        stage(odd, None, SWEEPS, t, last=True)
        stage(even, odd, SWEEPS - 1, t)

        @pl.loop(0, pairs - 1)
        def _(j):
            stage(odd, even, SWEEPS - 2 - 2 * j, t)
            stage(even, odd, SWEEPS - 3 - 2 * j, t)

        @pl.when(t < chunks)
        def _():
            first_stage(t)
            send(even, 0, t)

        pl.when(t == chunks)(lambda: settle(even, 0))

    if n_space > 1:
        pl.when(has_upper)(lambda: k_up().wait_send())
        pl.when(has_lower)(lambda: k_down().wait_send())

    @pl.loop(0, chunks)
    def _(b):
        for d in range(1, n_node):
            node_copy(d, b).wait_send()
        if n_tm > 1:
            pl.when(jnp.logical_not(last_tm))(lambda: prev_copy(b).wait_send())
        out_copy(b).wait()


def body(n_node, n_tm, n_space, nodes, prev_final, u_init, conductivity):
    per, bricks, height, width = nodes.shape[1:]
    chunks = height // ROWS
    field = (bricks, height, width)
    f32 = jnp.float32
    vmem = pltpu.VMEM
    dma = pltpu.SemaphoreType.DMA
    others = max(n_node - 1, 1)
    return pl.pallas_call(
        functools.partial(kernel, (n_node, n_tm, n_space, per, bricks, height)),
        out_shape=jax.ShapeDtypeStruct(nodes.shape, f32),
        in_specs=[pl.BlockSpec(memory_space=pl.ANY)] * 4,
        out_specs=pl.BlockSpec(memory_space=pl.ANY),
        scratch_shapes=[
            vmem((per,) + field, f32),
            vmem((others, per) + field, f32),
            vmem(field, f32),
            vmem((per, bricks + 2, height + 2 * PAD, width), f32),
            vmem((per, bricks + 2, height + 2 * PAD, width), f32),
            vmem((bricks + 2, height + 2 * PAD, width), f32),
            vmem((bricks + 1, height, width), f32),
            vmem(field, f32),
            vmem(field, f32),
            vmem(field, f32),
            vmem(field, f32),
            vmem((per,) + field, f32),
            vmem((per,) + field, f32),
            vmem((per,) + field, f32),
            dma((2,)),
            dma((2,)),
            dma((2,)),
            dma((others, chunks)),
            dma((others, chunks)),
            dma((chunks,)),
            dma((chunks,)),
            dma((2, SWEEPS)),
            dma((2, SWEEPS, chunks)),
            dma((chunks,)),
        ],
        compiler_params=pltpu.CompilerParams(
            collective_id=0, has_side_effects=True, vmem_limit_bytes=58 * 1024 * 1024
        ),
        name="sdc_sweep",
    )(nodes, prev_final, u_init, conductivity)


def solution(mesh):
    in_specs = (
        P("tm", "node", "space", None, None),
        P("tm", "space", None, None),
        P("space", None, None),
        P("space", None, None),
    )
    out_specs = P("tm", "node", "space", None, None)
    sized = functools.partial(body, mesh.shape["node"], mesh.shape["tm"], mesh.shape["space"])
    return jax.shard_map(sized, mesh=mesh, in_specs=in_specs, out_specs=out_specs, check_vma=False)
```

profile of v0, /device:TPU:1, one launch (start us, length us, event | category | flops | bytes accessed | tf_op | source)
XLA Modules:
  0.0 131.0 jit_solution(16655818313287119767)
XLA Ops:
  0.0 126.4 %sdc_sweep.1 = f32[1,2,8,256,256]{4,3,2,1,0:T(8,128)} custom-call(f32[1,2,8,256,256]{4,3,2,1,0:T(8,128)} %nodes.1, f32[1,8,256,256]{3,2,1,0:T(8,128)} %prev.1, f32[8,256,256]{2,1,0:T(8,128)} %init.1, f32[8,256,256]{2,1,0:T(8,128)} %cond.1), custom_call_target="tpu_custom_call" | custom-call | tf_op jit(solution)/shard_map/sdc_sweep/pallas_call | solution.py:353
  126.4 4.6 %copy.6 = f32[1,2,8,256,256]{4,3,2,1,0:T(8,128)} copy(f32[1,2,8,256,256]{4,3,2,1,0:T(8,128)} %sdc_sweep.1) | data formatting | bytes 8388608
where the time goes:
time: 131 us
  Pallas kernels  126 us (96%)
  local copies, waits for them, and re-layouts  4.6 us (4%)
    pallas_call x1, Pallas kernels, body(): pl.pallas_call(functools.partial(kernel, (n_node, n_tm, n_space, per, bri...  126 us
    unnamed x1, local copies, waits for them, and re-layouts  4.6 us

commit v1 on v0

--- a/solution.py
+++ b/solution.py
@@ -45,9 +45,9 @@
 
 def kernel(
     sizes, nodes, prev, init, cond, out,
-    own, theirs, start, even, odd, kpad, fx, fyl, fyr, fzl, fzr, inv, rhs, result,
+    own, theirs, start, even, odd, kpad, fx, fyl, fyr, fzl, fzr, inv, rhs,
     load_sem, k_send, k_recv, node_send, node_recv, prev_send, prev_recv,
-    halo_send, halo_recv, out_sem,
+    halo_send, halo_recv,
 ):
     n_node, n_tm, n_space, per, bricks, height = sizes
     chunks = height // ROWS
@@ -131,10 +131,6 @@
             buffer.at[:, 1, rows], buffer.at[:, bricks + 1, rows],
             halo_send.at[1, s], halo_recv.at[1, s, b],
             device_id={"space": lower}, device_id_type=MESH)
-
-    def out_copy(b):
-        rows = pl.ds(pl.multiple_of(b * ROWS, ROWS), ROWS)
-        return pltpu.make_async_copy(result.at[:, :, rows], out.at[0, :, :, rows], out_sem.at[b])
 
     own_load = pltpu.make_async_copy(nodes.at[0], own, load_sem.at[0])
     k_load = pltpu.make_async_copy(cond, kpad.at[pl.ds(1, bricks), inner], load_sem.at[1])
@@ -250,11 +246,11 @@
                 even[i, x + 1, inside] = mine[i] + q
                 rhs[i, x, rows] = (begin + q) * inv_point[i]
 
-    def sweep(src, dst, b, last):
+    def sweep(src, dst, b, last, planes):
         r = pl.multiple_of(b * ROWS, ROWS)
         rows = pl.ds(r, ROWS)
         inside = pl.ds(pl.multiple_of(r + PAD, 8), ROWS)
-        for x in range(bricks):
+        for x in planes:
             xl, xr = fx[x, rows], fx[x + 1, rows]
             yl, yr = fyl[x, rows], fyr[x, rows]
             zl, zr = fzl[x, rows], fzr[x, rows]
@@ -269,7 +265,7 @@
                 value = value + zr * pltpu.roll(centre, width - 1, 1)
                 value = (value + right) * inv[i, x, rows]
                 if last:
-                    result[i, x, rows] = value - (point[i] * right - start[x, rows])
+                    out[0, i, x, rows] = value - (point[i] * right - start[x, rows])
                 else:
                     dst[i, x + 1, inside] = value
 
@@ -296,38 +292,38 @@
             pl.when(has_lower)(lambda: halo_down(buffer, s, chunks - 1).wait_send())
 
     def stage(src, dst, s, t, last=False):
-        b = t - 2 * s
+        b = t - s
 
         @pl.when((b >= 0) & (b < chunks))
         def _():
             receive(src, s - 1, b)
-            sweep(src, dst, b, last)
             if last:
-                out_copy(b).start()
+                sweep(src, dst, b, last, range(bricks))
             else:
+                ends = sorted({0, bricks - 1})
+                sweep(src, dst, b, last, ends)
                 send(dst, s, b)
+                sweep(src, dst, b, last, range(1, bricks - 1))
 
         if not last:
             pl.when(b == chunks)(lambda: settle(dst, s))
 
-    pairs = SWEEPS // 2
-
-    @pl.loop(0, chunks + 2 * SWEEPS)
+    @pl.loop(0, chunks + SWEEPS)
     def _(t):
-        stage(odd, None, SWEEPS, t, last=True)
-        stage(even, odd, SWEEPS - 1, t)
-
-        @pl.loop(0, pairs - 1)
-        def _(j):
-            stage(odd, even, SWEEPS - 2 - 2 * j, t)
-            stage(even, odd, SWEEPS - 3 - 2 * j, t)
-
         @pl.when(t < chunks)
         def _():
             first_stage(t)
             send(even, 0, t)
 
         pl.when(t == chunks)(lambda: settle(even, 0))
+
+        @pl.loop(0, SWEEPS // 2 - 1)
+        def _(j):
+            stage(even, odd, 2 * j + 1, t)
+            stage(odd, even, 2 * j + 2, t)
+
+        stage(even, odd, SWEEPS - 1, t)
+        stage(odd, None, SWEEPS, t, last=True)
 
     if n_space > 1:
         pl.when(has_upper)(lambda: k_up().wait_send())
@@ -339,7 +335,6 @@
             node_copy(d, b).wait_send()
         if n_tm > 1:
             pl.when(jnp.logical_not(last_tm))(lambda: prev_copy(b).wait_send())
-        out_copy(b).wait()
 
 
 def body(n_node, n_tm, n_space, nodes, prev_final, u_init, conductivity):
@@ -352,9 +347,9 @@
     others = max(n_node - 1, 1)
     return pl.pallas_call(
         functools.partial(kernel, (n_node, n_tm, n_space, per, bricks, height)),
-        out_shape=jax.ShapeDtypeStruct(nodes.shape, f32),
-        in_specs=[pl.BlockSpec(memory_space=pl.ANY)] * 4,
-        out_specs=pl.BlockSpec(memory_space=pl.ANY),
+        out_shape=pltpu.VMEM(nodes.shape, f32),
+        in_specs=[pl.BlockSpec(memory_space=pltpu.HBM)] * 4,
+        out_specs=pl.BlockSpec(memory_space=pltpu.VMEM),
         scratch_shapes=[
             vmem((per,) + field, f32),
             vmem((others, per) + field, f32),
@@ -367,7 +362,6 @@
             vmem(field, f32),
             vmem(field, f32),
             vmem(field, f32),
-            vmem((per,) + field, f32),
             vmem((per,) + field, f32),
             vmem((per,) + field, f32),
             dma((2,)),
@@ -379,10 +373,9 @@
             dma((chunks,)),
             dma((2, SWEEPS)),
             dma((2, SWEEPS, chunks)),
-            dma((chunks,)),
         ],
         compiler_params=pltpu.CompilerParams(
-            collective_id=0, has_side_effects=True, vmem_limit_bytes=58 * 1024 * 1024
+            collective_id=0, has_side_effects=True, vmem_limit_bytes=48 * 1024 * 1024
         ),
         name="sdc_sweep",
     )(nodes, prev_final, u_init, conductivity)

time: 131 us -> 122 us (0.931)
  Pallas kernels: 126 us -> 120 us
  local copies, waits for them, and re-layouts: 4.6 us -> 2.02 us
    pallas_call x1, Pallas kernels: 126 us -> 120 us  [body(): pl.pallas_call(functools.partial(kernel, (n_node, n_tm, n_space, per, bri...]
    unnamed x1, local copies, waits for them, and re-layouts: 4.6 us -> 2.02 us
where the time goes in v1:
time: 122 us
  Pallas kernels  120 us (98%)
  local copies, waits for them, and re-layouts  2.02 us (2%)
    pallas_call x1, Pallas kernels, body(): pl.pallas_call(functools.partial(kernel, (n_node, n_tm, n_space, per, bri...  120 us

profile of v1, /device:TPU:1, one launch (start us, length us, event | category | flops | bytes accessed | tf_op | source)
XLA Modules:
  0.0 121.7 jit_solution(3282116820418734568)
XLA Ops:
  0.0 119.7 %sdc_sweep.1 = f32[1,2,8,256,256]{4,3,2,1,0:T(8,128)S(1)} custom-call(f32[1,2,8,256,256]{4,3,2,1,0:T(8,128)} %nodes.1, f32[1,8,256,256]{3,2,1,0:T(8,128)} %prev.1, f32[8,256,256]{2,1,0:T(8,128)} %init.1, f32[8,256,256]{2,1,0:T(8,128)} %cond.1), custom_call_target="tpu_custom_call" | custom-call | tf_op jit(solution)/shard_map/sdc_sweep/pallas_call | solution.py:348
  119.7 2.0 %copy.6 = f32[1,2,8,256,256]{4,3,2,1,0:T(8,128)} copy(f32[1,2,8,256,256]{4,3,2,1,0:T(8,128)S(1)} %sdc_sweep.1) | data formatting | bytes 8388608
